TPU v7x, 128 devices: a whole 4x4x4 slice. The times are simulated.
128 devices in a mesh: seq: 16 (over z, x_hi, core), exp: 8 (over y, x_lo).
Axes of the slice: x: 4 (x_hi: 2, x_lo: 2; x = x_hi * 2 + x_lo), y: 4, z: 4, core: 2. Of those that a mesh axis runs over, the one named last changes fastest.
Arguments:
- tokens: bfloat16 [524288, 1024], P(('seq', 'exp')), may hold values from -6 to 6
- norm_gain: float32 [1024], replicated, may hold values from 0.1 to 1.9
- slot_param: bfloat16 [1024, 256], replicated
- w_in: bfloat16 [64, 1024, 4096], P('exp', None, 'seq'), may hold values from -0.1875 to 0.1875
- w_out: bfloat16 [64, 4096, 1024], P('exp', 'seq'), may hold values from -0.09375 to 0.09375
Outputs:
- mixed: bfloat16 [524288, 1024], P(('seq', 'exp'))
All inputs are finite; a program needn't handle non-finite values.
Results may differ from a plain program's by a relative error of at most 0.02.
The roundings to bfloat16 on the way count: a program that leaves them out, or rounds other values in their place, can miss the bound.
Values may be sent and summed in bfloat16 or wider, within the bound.
A program may use at most 128 MiB of HBM per device.

v0:
```python
import jax
import jax.numpy as jnp
from jax import lax
from jax.sharding import PartitionSpec as P


def on_device(tokens, norm_gain, slot_param, w_in, w_out):
    n_exp = lax.axis_size("exp")
    slot_count = slot_param.shape[1]
    width = tokens.shape[1]
    group = slot_count // n_exp
    values = tokens.astype(jnp.float32)
    scale = lax.rsqrt(jnp.mean(values * values, axis=1, keepdims=True) + 1e-06)
    normed = (values * scale * norm_gain[None, :]).astype(jnp.bfloat16)
    logits = jnp.dot(normed, slot_param, preferred_element_type=jnp.float32)
    col_peak = lax.pmax(jnp.max(logits, axis=0), ("seq", "exp"))
    raw = jnp.exp(logits - col_peak[None, :])
    dispatch = raw.astype(jnp.bfloat16)
    weighted = lax.dot_general(
        dispatch, normed, (((0,), (0,)), ((), ())), preferred_element_type=jnp.float32
    )
    col_total = jnp.sum(raw, axis=0)
    group_sum, group_total = (
        lax.psum_scatter(weighted, "exp", scatter_dimension=0, tiled=True),
        lax.psum_scatter(col_total, "exp", scatter_dimension=0, tiled=True),
    )
    group_sum, group_total = lax.psum((group_sum, group_total), "seq")
    slot_in = (group_sum / group_total[:, None]).astype(jnp.bfloat16)
    local_experts = w_in.shape[0]
    grouped = slot_in.reshape(local_experts, group // local_experts, width)
    first = jnp.einsum("esd,edh->esh", grouped, w_in, preferred_element_type=jnp.float32)
    hidden_act = jax.nn.gelu(first, approximate=False).astype(jnp.bfloat16)
    partial_out = jnp.einsum(
        "esh,ehd->esd", hidden_act, w_out, preferred_element_type=jnp.float32
    ).reshape(group, width)
    group_out = lax.psum(partial_out.astype(jnp.bfloat16), "seq")
    slot_out = lax.all_gather(group_out, "exp", axis=0, tiled=True)
    row_peak = jnp.max(logits, axis=1, keepdims=True)
    expon = jnp.exp(logits - row_peak)
    combine = (expon / jnp.sum(expon, axis=1, keepdims=True)).astype(jnp.bfloat16)
    return jnp.dot(combine, slot_out, preferred_element_type=jnp.float32).astype(jnp.bfloat16)


def solution(mesh):
    in_specs = (P(("seq", "exp"), None), P(), P(), P("exp", None, "seq"), P("exp", "seq", None))
    out_specs = P(("seq", "exp"), None)
    return jax.shard_map(
        on_device, mesh=mesh, in_specs=in_specs, out_specs=out_specs, check_vma=False
    )
```

profile of v0, /device:TPU:0, one launch (start us, length us, event | category | flops | bytes accessed | tf_op | source)
XLA Modules:
  0.0 451.9 jit_solution(9162732727968139499)
XLA Ops:
  6.5 0.0 copy-start
  6.5 0.0 copy-start.3
  6.5 0.0 reduce-scatter.2.cloned.1.call-start
  6.5 5.2 %fusion = f32[4096]{0:T(1024)S(1)} fusion(bf16[4096,1024]{1,0:T(8,128)(2,1)} %param.5), kind=kLoop, calls=%fused_computation.2 | loop fusion | flops 12578816 | bytes 8404992 | tf_op jit(solution)/shard_map/reduce_sum | solution.py:13
  11.8 0.0 copy-done
  11.8 0.0 copy-done.3
  11.8 0.7 copy-done.1
  12.5 5.2 %fusion.89 = (f32[4096]{0:T(1024)S(1)}, f32[256]{0:T(256)S(1)}, f32[4096,256]{1,0:T(8,128)}) fusion(bf16[1024,256]{1,0:T(8,128)(2,1)S(1)} %copy-done, bf16[4096,1024]{1,0:T(8,128)(2,1)S(1)} %copy-done.1, f32[1024]{0:T(1024)S(1)} %copy-done.3, f32[4096]{0:T(1024)S(1)} %add_rsqrt_fusion), kind=kOutput, calls=%fused_computation.106 | convolution fusion | flops 2166353664 | bytes 13145088 | tf_op jit(solution)/shard_map/dot_general | solution.py:15
  17.7 68.2 %pmax.7 = f32[256]{0:T(256)S(1)} all-reduce(f32[256]{0:T(256)S(1)} %get-tuple-element.8), channel_id=1, replica_groups=mesh['seq'=16,'exp'=8] {'seq','exp'}, use_global_device_ids=true, to_apply=%region_4.0 | all-reduce | flops 256 | bytes 2048 | tf_op jit(solution)/shard_map/pmax | solution.py:16
  85.9 8.9 %fusion.6 = f32[256,1024]{1,0:T(8,128)} fusion(bf16[4096,1024]{1,0:T(8,128)(2,1)} %param.5, f32[1024]{0:T(1024)S(1)} %copy-done.3, f32[4096]{0:T(1024)S(1)} %add_rsqrt_fusion, f32[4096,256]{1,0:T(8,128)} %get-tuple-element.11, f32[256]{0:T(256)S(1)} %pmax.7), kind=kOutput, calls=%fused_computation.12 | convolution fusion | flops 2166358016 | bytes 13652992 | tf_op jit(solution)/shard_map/dot_general | solution.py:19
  94.8 0.0 reduce-scatter.2.cloned.1.call-update
  94.8 0.0 all-reduce.4.cloned.1.call-start
  94.8 37.9 %reduce-scatter.2.cloned.1.call-done = f32[32,1024]{1,0:T(8,128)} async-done(((f32[256,1024]{1,0:T(8,128)}), f32[32,1024]{1,0:T(8,128)}) %reduce-scatter.2.cloned.1.call-update) | async-done | bytes 131088 | tf_op jit(solution)/shard_map/reduce_scatter | solution.py:24
  132.7 0.0 all-reduce.4.cloned.1.call-update
  132.8 0.0 all-reduce.6.cloned.1.call-start
  132.8 3.4 fusion.3
  136.2 0.0 copy-done.4
  136.2 0.6 dynamic-slice
  137.4 16.9 %all-reduce = f32[256]{0:T(256)S(1)} all-reduce(f32[256]{0:T(256)S(1)} %get-tuple-element.6), channel_id=3, replica_groups=mesh['seq'=16,'exp'=8] {'exp'}, use_global_device_ids=true, to_apply=%region_8.0.clone | all-reduce | flops 256 | bytes 2048
  154.4 0.1 dynamic-slice.1
  154.4 33.1 %psum.22 = f32[32]{0:T(128)S(1)} all-reduce(f32[32]{0:T(128)S(1)} %dynamic-slice.1), channel_id=1, replica_groups=mesh['seq'=16,'exp'=8] {'seq'}, use_global_device_ids=true, to_apply=%region_9.0 | all-reduce | flops 32 | bytes 256 | tf_op jit(solution)/shard_map/psum | solution.py:27
  187.6 85.0 %all-reduce.4.cloned.1.call-done = f32[32,1024]{1,0:T(8,128)} async-done(((f32[32,1024]{1,0:T(8,128)}), f32[32,1024]{1,0:T(8,128)}) %all-reduce.4.cloned.1.call-update) | async-done | bytes 131088 | tf_op jit(solution)/shard_map/psum | solution.py:27
  272.5 1.0 divide_convert_fusion.2
  273.6 0.0 copy-start.2
  273.6 3.0 fusion.55
  276.6 0.4 copy-done.2
  277.0 0.7 convolution_convert_fusion.1
  277.7 0.7 convert_element_type.34
  278.3 0.0 all-reduce.6.cloned.1.call-update
  278.4 130.1 %all-reduce.6.cloned.1.call-done = bf16[32,1024]{1,0:T(8,128)(2,1)} async-done(((bf16[32,1024]{1,0:T(8,128)(2,1)}), bf16[32,1024]{1,0:T(8,128)(2,1)}) %all-reduce.6.cloned.1.call-update) | async-done | bytes 65552 | tf_op jit(solution)/shard_map/psum | solution.py:36
  408.5 30.5 %all_gather.3 = bf16[256,1024]{1,0:T(8,128)(2,1)S(1)} all-gather(bf16[32,1024]{1,0:T(8,128)(2,1)} %all-reduce.6.cloned.1.call-done), channel_id=1, replica_groups=mesh['seq'=16,'exp'=8] {'exp'}, dimensions={0}, use_global_device_ids=true | all-gather | bytes 589824 | tf_op jit(solution)/shard_map/all_gather | solution.py:37
  439.0 6.4 %convolution_convert_fusion = bf16[4096,1024]{1,0:T(8,128)(2,1)} fusion(bf16[256,1024]{1,0:T(8,128)(2,1)S(1)} %all_gather.3, f32[4096,256]{1,0:T(8,128)} %get-tuple-element.11, f32[4096]{0:T(1024)S(1)} %get-tuple-element.5, f32[4096]{0:T(1024)S(1)} %get-tuple-element.7), kind=kOutput, calls=%fused_computation.5 | convolution fusion | flops 2154823680 | bytes 13139968 | tf_op jit(solution)/shard_map/dot_general | solution.py:41
  (4 shorter events, 0.0 us)
Async XLA Ops:
  6.5 5.3 %copy-start = (bf16[1024,256]{1,0:T(8,128)(2,1)S(1)}, bf16[1024,256]{1,0:T(8,128)(2,1)}, u32[]{:S(2)}) copy-start(bf16[1024,256]{1,0:T(8,128)(2,1)} %param.7) | copy-start | bytes 1572868
  6.5 5.3 %copy-start.3 = (f32[1024]{0:T(1024)S(1)}, f32[1024]{0:T(1024)}, u32[]{:S(2)}) copy-start(f32[1024]{0:T(1024)} %param.6) | copy-start | bytes 12292
  6.5 126.2 %reduce-scatter.2.cloned.1.call-start = ((), (), s32[]{:S(2)}) async-start(), calls=%async_computation.1 | async-start | bytes 1179648 | tf_op jit(solution)/shard_map/reduce_scatter | solution.py:24
  6.5 6.0 %copy-start.1 = (bf16[4096,1024]{1,0:T(8,128)(2,1)S(1)}, bf16[4096,1024]{1,0:T(8,128)(2,1)}, u32[]{:S(2)}) copy-start(bf16[4096,1024]{1,0:T(8,128)(2,1)} %param.5) | copy-start | bytes 25165828
  94.8 41.4 %copy-start.4 = (u32[128]{0:T(128)S(1)}, u32[128]{0:T(128)}, u32[]{:S(2)}) copy-start(u32[128]{0:T(128)} %constant.70) | copy-start | bytes 1540
  94.8 177.8 %all-reduce.4.cloned.1.call-start = ((), (), s32[]{:S(2)}) async-start(), calls=%async_computation.2 | async-start | bytes 262144 | tf_op jit(solution)/shard_map/psum | solution.py:27
  132.8 275.7 %all-reduce.6.cloned.1.call-start = ((), (), s32[]{:S(2)}) async-start(), calls=%async_computation.3 | async-start | bytes 131072 | tf_op jit(solution)/shard_map/psum | solution.py:36
  273.6 3.5 copy-start.2
Sparse Core Ops, SparseCore 0:
  94.9 37.7 reduce-scatter.1
  135.2 137.2 all-reduce.3
  278.5 129.9 all-reduce.5
where the time goes:
time: 452 us
  waiting for transfers between devices  253 us (56%)
  blocking collectives  149 us (33%)
  matrix products  24.2 us (5%)
  between operations  13.8 us (3%)
  other arithmetic  9.59 us (2%)
    psum x1, waiting for transfers between devices, on_device(): group_out = lax.psum(partial_out.astype(jnp.bfloat16), 'seq')  130 us
    psum x1, waiting for transfers between devices, on_device(): group_sum, group_total = lax.psum((group_sum, group_total), 'seq')  85 us
    pmax x1, blocking collectives, on_device(): col_peak = lax.pmax(jnp.max(logits, axis=0), ('seq', 'exp'))  68.2 us
    reduce_scatter x1, waiting for transfers between devices, on_device(): lax.psum_scatter(weighted, 'exp', scatter_dimension=0, tiled=True)  37.9 us
    psum x1, blocking collectives, on_device(): group_sum, group_total = lax.psum((group_sum, group_total), 'seq')  33.1 us
    all_gather x1, blocking collectives, on_device(): slot_out = lax.all_gather(group_out, 'exp', axis=0, tiled=True)  30.5 us
    unnamed x1, blocking collectives  16.9 us
  transfers between devices with their start and end apart: 3, of which 3 were waited for; matrix products, arithmetic and copies ran while one was open for 1% of the time, Pallas kernels for 0%

commit v1 on v0

--- a/solution.py
+++ b/solution.py
@@ -2,6 +2,13 @@
 import jax.numpy as jnp
 from jax import lax
 from jax.sharding import PartitionSpec as P
+
+
+def swapped_in(x, name, dim):
+    size = lax.axis_size(name)
+    pieces = jnp.stack([x for _ in range(size)])
+    pieces = lax.all_to_all(pieces, name, split_axis=0, concat_axis=0)
+    return jnp.concatenate(pieces, axis=dim)
 
 
 def on_device(tokens, norm_gain, slot_param, w_in, w_out):
@@ -34,7 +41,7 @@
         "esh,ehd->esd", hidden_act, w_out, preferred_element_type=jnp.float32
     ).reshape(group, width)
     group_out = lax.psum(partial_out.astype(jnp.bfloat16), "seq")
-    slot_out = lax.all_gather(group_out, "exp", axis=0, tiled=True)
+    slot_out = swapped_in(group_out, "exp", 0)
     row_peak = jnp.max(logits, axis=1, keepdims=True)
     expon = jnp.exp(logits - row_peak)
     combine = (expon / jnp.sum(expon, axis=1, keepdims=True)).astype(jnp.bfloat16)

time: 452 us -> 436 us (0.965)
  blocking collectives: 149 us -> 132 us
    all_gather x1 -> x0, blocking collectives: 30.5 us -> none  [on_device(): slot_out = lax.all_gather(group_out, 'exp', axis=0, tiled=True)]
    all_to_all x0 -> x1, blocking collectives: none -> 13.8 us  [swapped_in(): pieces = lax.all_to_all(pieces, name, split_axis=0, concat_axis=0)]
where the time goes in v1:
time: 436 us
  waiting for transfers between devices  253 us (58%)
  blocking collectives  132 us (30%)
  matrix products  24.2 us (6%)
  between operations  13.8 us (3%)
  other arithmetic  9.59 us (2%)
    psum x1, waiting for transfers between devices, on_device(): group_out = lax.psum(partial_out.astype(jnp.bfloat16), 'seq')  130 us
    psum x1, waiting for transfers between devices, on_device(): group_sum, group_total = lax.psum((group_sum, group_total), 'seq')  85 us
    pmax x1, blocking collectives, on_device(): col_peak = lax.pmax(jnp.max(logits, axis=0), ('seq', 'exp'))  68.2 us
    reduce_scatter x1, waiting for transfers between devices, on_device(): lax.psum_scatter(weighted, 'exp', scatter_dimension=0, tiled=True)  37.9 us
    psum x1, blocking collectives, on_device(): group_sum, group_total = lax.psum((group_sum, group_total), 'seq')  33.1 us
    unnamed x1, blocking collectives  16.9 us
    all_to_all x1, blocking collectives, swapped_in(): pieces = lax.all_to_all(pieces, name, split_axis=0, concat_axis=0)  13.8 us
    dot_general x1, matrix products, on_device(): lax.dot_general(dispatch, normed, (((0,), (0,)), ((), ())), preferred_ele...  8.9 us
  transfers between devices with their start and end apart: 3, of which 3 were waited for; matrix products, arithmetic and copies ran while one was open for 1% of the time, Pallas kernels for 0%

profile of v1, /device:TPU:0, one launch (start us, length us, event | category | flops | bytes accessed | tf_op | source)
XLA Modules:
  0.0 436.1 jit_solution(12407074653752215523)
XLA Ops:
  6.5 0.0 copy-start
  6.5 0.0 reduce-scatter.2.cloned.1.call-start
  6.5 5.2 %fusion = f32[4096]{0:T(1024)S(1)} fusion(bf16[4096,1024]{1,0:T(8,128)(2,1)} %param.5), kind=kLoop, calls=%fused_computation.2 | loop fusion | flops 12578816 | bytes 8404992 | tf_op jit(solution)/shard_map/reduce_sum | solution.py:20
  11.8 0.0 copy-done
  11.8 0.0 copy-done.3
  11.8 0.7 copy-done.1
  12.5 5.2 %fusion.89 = (f32[4096]{0:T(1024)S(1)}, f32[256]{0:T(256)S(1)}, f32[4096,256]{1,0:T(8,128)}) fusion(bf16[1024,256]{1,0:T(8,128)(2,1)S(1)} %copy-done, bf16[4096,1024]{1,0:T(8,128)(2,1)S(1)} %copy-done.1, f32[1024]{0:T(1024)S(1)} %copy-done.3, f32[4096]{0:T(1024)S(1)} %add_rsqrt_fusion), kind=kOutput, calls=%fused_computation.106 | convolution fusion | flops 2166353664 | bytes 13145088 | tf_op jit(solution)/shard_map/dot_general | solution.py:22
  17.7 68.2 %pmax.7 = f32[256]{0:T(256)S(1)} all-reduce(f32[256]{0:T(256)S(1)} %get-tuple-element.8), channel_id=1, replica_groups=mesh['seq'=16,'exp'=8] {'seq','exp'}, use_global_device_ids=true, to_apply=%region_4.0 | all-reduce | flops 256 | bytes 2048 | tf_op jit(solution)/shard_map/pmax | solution.py:23
  85.9 8.9 %fusion.6 = f32[256,1024]{1,0:T(8,128)} fusion(bf16[4096,1024]{1,0:T(8,128)(2,1)} %param.5, f32[1024]{0:T(1024)S(1)} %copy-done.3, f32[4096]{0:T(1024)S(1)} %add_rsqrt_fusion, f32[4096,256]{1,0:T(8,128)} %get-tuple-element.11, f32[256]{0:T(256)S(1)} %pmax.7), kind=kOutput, calls=%fused_computation.12 | convolution fusion | flops 2166358016 | bytes 13652992 | tf_op jit(solution)/shard_map/dot_general | solution.py:26
  94.8 0.0 reduce-scatter.2.cloned.1.call-update
  94.8 0.0 all-reduce.4.cloned.1.call-start
  94.8 37.9 %reduce-scatter.2.cloned.1.call-done = f32[32,1024]{1,0:T(8,128)} async-done(((f32[256,1024]{1,0:T(8,128)}), f32[32,1024]{1,0:T(8,128)}) %reduce-scatter.2.cloned.1.call-update) | async-done | bytes 131088 | tf_op jit(solution)/shard_map/reduce_scatter | solution.py:31
  132.7 0.0 all-reduce.4.cloned.1.call-update
  132.8 0.0 all-reduce.6.cloned.1.call-start
  132.8 3.4 fusion.3
  136.2 0.0 copy-done.4
  136.2 0.6 dynamic-slice
  137.4 16.9 %all-reduce = f32[256]{0:T(256)S(1)} all-reduce(f32[256]{0:T(256)S(1)} %get-tuple-element.6), channel_id=3, replica_groups=mesh['seq'=16,'exp'=8] {'exp'}, use_global_device_ids=true, to_apply=%region_8.0.clone | all-reduce | flops 256 | bytes 2048
  154.4 0.1 dynamic-slice.1
  154.4 33.1 %psum.22 = f32[32]{0:T(128)S(1)} all-reduce(f32[32]{0:T(128)S(1)} %dynamic-slice.1), channel_id=1, replica_groups=mesh['seq'=16,'exp'=8] {'seq'}, use_global_device_ids=true, to_apply=%region_9.0 | all-reduce | flops 32 | bytes 256 | tf_op jit(solution)/shard_map/psum | solution.py:34
  187.6 85.0 %all-reduce.4.cloned.1.call-done = f32[32,1024]{1,0:T(8,128)} async-done(((f32[32,1024]{1,0:T(8,128)}), f32[32,1024]{1,0:T(8,128)}) %all-reduce.4.cloned.1.call-update) | async-done | bytes 131088 | tf_op jit(solution)/shard_map/psum | solution.py:34
  272.5 1.0 divide_convert_fusion.2
  273.6 0.0 copy-start.2
  273.6 3.0 fusion.55
  276.6 0.4 copy-done.2
  277.0 0.7 convolution_convert_fusion.1
  277.7 0.7 convert_element_type.34
  278.3 0.0 all-reduce.6.cloned.1.call-update
  278.4 130.1 %all-reduce.6.cloned.1.call-done = bf16[32,1024]{1,0:T(8,128)(2,1)} async-done(((bf16[32,1024]{1,0:T(8,128)(2,1)}), bf16[32,1024]{1,0:T(8,128)(2,1)}) %all-reduce.6.cloned.1.call-update) | async-done | bytes 65552 | tf_op jit(solution)/shard_map/psum | solution.py:43
  408.5 0.9 stack.2
  409.3 13.8 %all_to_all.5 = bf16[8,32,1024]{2,1,0:T(8,128)(2,1)S(1)} all-to-all(bf16[8,32,1024]{2,1,0:T(8,128)(2,1)S(1)} %stack.2), channel_id=1, replica_groups=mesh['seq'=16,'exp'=8] {'exp'}, dimensions={0} | all-to-all | bytes 1048576 | tf_op jit(solution)/shard_map/all_to_all | solution.py:10
  423.1 6.4 %convolution_convert_fusion = bf16[4096,1024]{1,0:T(8,128)(2,1)} fusion(bf16[256,1024]{1,0:T(8,128)(2,1)S(1)} %bitcast.7, f32[4096,256]{1,0:T(8,128)} %get-tuple-element.11, f32[4096]{0:T(1024)S(1)} %get-tuple-element.5, f32[4096]{0:T(1024)S(1)} %get-tuple-element.7), kind=kOutput, calls=%fused_computation.5 | convolution fusion | flops 2154823680 | bytes 13139968 | tf_op jit(solution)/shard_map/dot_general | solution.py:48
  (5 shorter events, 0.0 us)
Async XLA Ops:
  6.5 5.3 %copy-start = (bf16[1024,256]{1,0:T(8,128)(2,1)S(1)}, bf16[1024,256]{1,0:T(8,128)(2,1)}, u32[]{:S(2)}) copy-start(bf16[1024,256]{1,0:T(8,128)(2,1)} %param.7) | copy-start | bytes 1572868
  6.5 5.3 %copy-start.3 = (f32[1024]{0:T(1024)S(1)}, f32[1024]{0:T(1024)}, u32[]{:S(2)}) copy-start(f32[1024]{0:T(1024)} %param.6) | copy-start | bytes 12292
  6.5 126.2 %reduce-scatter.2.cloned.1.call-start = ((), (), s32[]{:S(2)}) async-start(), calls=%async_computation.2 | async-start | bytes 1179648 | tf_op jit(solution)/shard_map/reduce_scatter | solution.py:31
  6.5 6.0 %copy-start.1 = (bf16[4096,1024]{1,0:T(8,128)(2,1)S(1)}, bf16[4096,1024]{1,0:T(8,128)(2,1)}, u32[]{:S(2)}) copy-start(bf16[4096,1024]{1,0:T(8,128)(2,1)} %param.5) | copy-start | bytes 25165828
  94.8 41.4 %copy-start.4 = (u32[128]{0:T(128)S(1)}, u32[128]{0:T(128)}, u32[]{:S(2)}) copy-start(u32[128]{0:T(128)} %constant.70) | copy-start | bytes 1540
  94.8 177.8 %all-reduce.4.cloned.1.call-start = ((), (), s32[]{:S(2)}) async-start(), calls=%async_computation.3 | async-start | bytes 262144 | tf_op jit(solution)/shard_map/psum | solution.py:34
  132.8 275.7 %all-reduce.6.cloned.1.call-start = ((), (), s32[]{:S(2)}) async-start(), calls=%async_computation.4 | async-start | bytes 131072 | tf_op jit(solution)/shard_map/psum | solution.py:43
  273.6 3.5 copy-start.2
Sparse Core Ops, SparseCore 0:
  94.9 37.7 reduce-scatter.1
  135.2 137.2 all-reduce.3
  278.5 129.9 all-reduce.5
